TPU v7x, 128 devices: a whole 4x4x4 slice. The times are simulated.
128 devices in a mesh: prow: 8 (over x, core), pcol: 16 (over z, y).
Axes of the slice: x: 4, y: 4, z: 4, core: 2. Of those that a mesh axis runs over, the one named last changes fastest.
Arguments:
- child_u: bfloat16 [2, 5, 8, 2, 16, 512, 128], P(None, None, 'prow', None, 'pcol'), may hold values from -5 to 5
- child_v: bfloat16 [2, 5, 8, 2, 16, 512, 128], P(None, None, 'prow', None, 'pcol'), may hold values from -5 to 5
- child_rank: int32 [2, 5, 8, 2, 16], P(None, None, 'prow', None, 'pcol'), may hold values from 0 to 128, as said below
- diag_shift: float32 [32, 512], replicated, may hold values from 0.5 to 4
Outputs:
- front_out: float32 [5, 8, 512, 2, 16, 512], P(None, 'prow', None, None, 'pcol')
Inputs may be any that keep to these rules, and one draw needn't show every extreme that they name: `child_rank`: 0 on and above the block diagonal (i <= j); below it 0 where the child has no tile, else from 16 to 128.
All inputs are finite; a program needn't handle non-finite values.
Results may differ from a plain program's by a relative error of at most 0.0003.
Values may be sent and summed in bfloat16 or wider, within the bound.
No kernel may reach another device: no remote copies, remote signals or barrier semaphores. Data moves between devices by JAX's collectives and lax.ppermute only.
A program may use at most 320 MiB of HBM per device.

v0:
```python
import jax
import jax.numpy as jnp
from jax import lax
from jax.sharding import PartitionSpec as P

PANELS = 2


def from_root(value, axis, root):
    return lax.dynamic_index_in_dim(lax.all_gather(value, axis), root, 0, keepdims=False)


def spread(value, axis, root):
    mine = lax.axis_index(axis) == root
    return lax.psum(jnp.where(mine, value, jnp.zeros_like(value)), axis)


def rows_for(lines, size):
    spare = -len(lines) % size
    return jnp.pad(lines, [(0, spare)] + [(0, 0)] * (lines.ndim - 1))


def sum_by_parts(value, axis):
    lines = value.reshape(-1, *value.shape[1:][-1:])
    padded = rows_for(lines, lax.axis_size(axis))
    own = lax.psum_scatter(padded, axis, scatter_dimension=0, tiled=True)
    whole = lax.all_gather(own, axis, axis=0, tiled=True)
    return whole[: len(lines)].reshape(value.shape)


def factor_panel(column, panel_index, block_rows, block_cols, own_column, prow_count, pcol_count):
    extent = column.shape[-1]
    pivot_tile = from_root(column[panel_index // prow_count], "prow", panel_index % prow_count)
    is_owner = own_column == panel_index % pcol_count
    pivot_tile = jnp.where(is_owner, pivot_tile, jnp.eye(extent, dtype=jnp.float32))
    factor = jnp.linalg.cholesky(pivot_tile)
    solved = lax.linalg.triangular_solve(
        factor, column.reshape(-1, extent), left_side=False, lower=True, transpose_a=True
    ).reshape(column.shape)
    below_mask = (block_rows > panel_index)[:, None, None]
    solved = jnp.where(below_mask, solved, 0.0)
    pivot_diag = jnp.diagonal(factor)
    at_pivot = (block_rows == panel_index)[:, None, None]
    panel_out = jnp.where(
        at_pivot, (factor * pivot_diag[None, :])[None], solved * pivot_diag[None, None, :]
    )
    rounded = solved.astype(jnp.bfloat16)
    received = spread(rounded, "pcol", panel_index % pcol_count)
    picked = jnp.take(received, block_cols // prow_count, axis=0)
    column_rows = from_root(picked, "prow", own_column % prow_count)
    return (received, column_rows, panel_out, is_owner)


def trailing(column, received, other_rows):
    return column - jnp.einsum(
        "rab,cb->rac", received, other_rows, preferred_element_type=jnp.float32
    )


def on_device(child_u, child_v, child_rank, diag_shift):
    prow_count = lax.axis_size("prow")
    pcol_count = lax.axis_size("pcol")
    own_row = lax.axis_index("prow")
    own_column = lax.axis_index("pcol")
    rank_grid = child_rank[:, :, 0, :, 0]
    rows_here = rank_grid.shape[1]
    cols_here = rank_grid.shape[2]
    extent = child_u.shape[-2]
    keep_mask = (
        jnp.arange(child_u.shape[-1], dtype=jnp.int32)[None, None, None, :]
        < rank_grid[:, :, :, None]
    ).astype(jnp.bfloat16)
    left_factor = child_u[:, :, 0, :, 0] * keep_mask[:, :, :, None, :]
    right_factor = child_v[:, :, 0, :, 0] * keep_mask[:, :, :, None, :]
    tile_grid = jnp.einsum(
        "crtak,crtbk->rtab", left_factor, right_factor, preferred_element_type=jnp.float32
    )
    row_terms = jnp.einsum(
        "crtak,crtbk->rab", left_factor, left_factor, preferred_element_type=jnp.float32
    )
    column_terms = jnp.einsum(
        "crtak,crtbk->tab", right_factor, right_factor, preferred_element_type=jnp.float32
    )
    row_sums = sum_by_parts(row_terms, "pcol")
    column_sums = lax.psum(column_terms, "prow")
    block_rows = jnp.arange(rows_here, dtype=jnp.int32) * prow_count + own_row
    block_cols = jnp.arange(cols_here, dtype=jnp.int32) * pcol_count + own_column
    slab_total = diag_shift.shape[0]
    select_cols = (block_cols[:, None] == jnp.arange(slab_total, dtype=jnp.int32)[None, :]).astype(
        jnp.float32
    )
    shift_cols = jnp.dot(select_cols, diag_shift, precision=lax.Precision.HIGHEST)
    identity = jnp.eye(extent, dtype=jnp.float32)
    diag_terms = (
        row_sums[:, None]
        + column_sums[None, :]
        + identity[None, None] * shift_cols[None, :, None, :]
    )
    on_diagonal = (block_rows[:, None] == block_cols[None, :])[:, :, None, None]
    tile_grid = tile_grid + jnp.where(on_diagonal, diag_terms, 0.0)
    columns = [tile_grid[:, column_index] for column_index in range(cols_here)]
    results = [jnp.zeros_like(columns[0]) for column_index in range(cols_here)]
    for panel_index in range(PANELS):
        local_col = panel_index // pcol_count
        received, column_rows, panel_out, is_owner = factor_panel(
            columns[local_col],
            panel_index,
            block_rows,
            block_cols,
            own_column,
            prow_count,
            pcol_count,
        )
        results[local_col] = jnp.where(is_owner, panel_out, results[local_col])
        columns = [
            trailing(columns[column_index], received, column_rows[column_index])
            for column_index in range(cols_here)
        ]
    outputs = []
    for column_index in range(cols_here):
        lower_mask = (block_rows >= block_cols[column_index])[:, None, None]
        finished = jnp.where(lower_mask, columns[column_index], 0.0)
        outputs.append(
            jnp.where(block_cols[column_index] < PANELS, results[column_index], finished)
        )
    stacked = jnp.stack(outputs, axis=1)
    return stacked.transpose(0, 2, 1, 3)[:, None, :, :, None, :]


def solution(mesh):
    placed = (
        P(None, None, "prow", None, "pcol", None, None),
        P(None, None, "prow", None, "pcol", None, None),
        P(None, None, "prow", None, "pcol"),
        P(),
    )
    return jax.shard_map(
        on_device,
        mesh=mesh,
        in_specs=placed,
        out_specs=P(None, "prow", None, None, "pcol", None),
        check_vma=False,
    )
```

profile of v0, /device:TPU:1, one launch (start us, length us, event | category | flops | bytes accessed | tf_op | source)
XLA Modules:
  0.0 967.2 jit_solution(4222597804145825684)
XLA Ops:
  8.3 6.5 fusion.31
  19.5 76.8 %reduce-scatter.2.cloned.1.call-done = f32[160,512]{1,0:T(8,128)} async-done(((f32[2560,512]{1,0:T(8,128)}), f32[160,512]{1,0:T(8,128)}) %reduce-scatter.2.cloned.1.call-update) | async-done | bytes 327696 | tf_op jit(solution)/shard_map/reduce_scatter | solution.py:26
  103.6 5.7 fusion.32
  109.2 46.1 %all-gather.9.cloned.1.call-done = f32[2560,512]{1,0:T(8,128)} async-done(((f32[160,512]{1,0:T(8,128)}), f32[2560,512]{1,0:T(8,128)}) %all-gather.9.cloned.1.call-update) | async-done | bytes 5242896 | tf_op jit(solution)/shard_map/all_gather | solution.py:27
  155.3 7.9 bitcast_add_fusion
  163.2 4.1 copy-done.2
  168.6 5.9 slice.199
  174.5 43.5 %all-gather.13.cloned.1.call-done = f32[8,1,512,512]{3,2,1,0:T(8,128)} async-done(((f32[1,1,512,512]{3,2,1,0:T(8,128)}), f32[8,1,512,512]{3,2,1,0:T(8,128)}) %all-gather.13.cloned.1.call-update) | async-done | bytes 8388624 | tf_op jit(solution)/shard_map/all_gather | solution.py:10
  220.3 11.7 %cholesky.286 = f32[128,128]{1,0:T(8,128)S(1)} custom-call(f32[128,128]{1,0:T(8,128)S(1)} %cholesky.426), custom_call_target="Cholesky" | custom-call | tf_op jit(solution)/shard_map/jit(cholesky)/cholesky | solution.py:36
  232.1 9.8 %custom-call.31 = f32[1,128,128]{1,2,0:T(8,128)S(1)} custom-call(f32[1,128,128]{2,1,0:T(8,128)S(1)} %get-tuple-element.67), custom_call_target="InvertDiagBlocksLowerTriangular" | custom-call | tf_op jit(solution)/shard_map/jit(cholesky)/cholesky | solution.py:36
  244.5 11.7 %cholesky.305 = f32[128,128]{1,0:T(8,128)S(1)} custom-call(f32[128,128]{1,0:T(8,128)S(1)} %cholesky.430), custom_call_target="Cholesky" | custom-call | tf_op jit(solution)/shard_map/jit(cholesky)/cholesky | solution.py:36
  256.2 10.3 %custom-call.32 = f32[1,128,128]{1,2,0:T(8,128)S(1)} custom-call(f32[1,128,128]{2,1,0:T(8,128)S(1)} %get-tuple-element.64), custom_call_target="InvertDiagBlocksLowerTriangular" | custom-call | tf_op jit(solution)/shard_map/jit(cholesky)/cholesky | solution.py:36
  268.1 11.7 %cholesky.326 = f32[128,128]{1,0:T(8,128)S(1)} custom-call(f32[128,128]{1,0:T(8,128)S(1)} %cholesky.435), custom_call_target="Cholesky" | custom-call | tf_op jit(solution)/shard_map/jit(cholesky)/cholesky | solution.py:36
  279.8 9.8 %custom-call.33 = f32[1,128,128]{1,2,0:T(8,128)S(1)} custom-call(f32[1,128,128]{2,1,0:T(8,128)S(1)} %get-tuple-element.61), custom_call_target="InvertDiagBlocksLowerTriangular" | custom-call | tf_op jit(solution)/shard_map/jit(cholesky)/cholesky | solution.py:36
  291.1 11.9 %cholesky.343 = f32[128,128]{1,0:T(8,128)S(1)} custom-call(f32[128,128]{1,0:T(8,128)S(1)} %convolution_subtract_fusion.9), custom_call_target="Cholesky" | custom-call | tf_op jit(solution)/shard_map/jit(cholesky)/cholesky | solution.py:36
  308.9 8.4 while.4
  317.3 39.3 %custom-call.34 = f32[4,128,128]{1,2,0:T(8,128)S(1)} custom-call(f32[4,128,128]{2,1,0:T(8,128)S(1)} %get-tuple-element.22), custom_call_target="InvertDiagBlocksLowerTriangular" | custom-call | tf_op jit(solution)/shard_map/triangular_solve/custom-call.3 | solution.py:37
  359.4 3.5 convolution_subtract_fusion.1
  364.3 4.4 convolution_subtract_fusion.3
  370.0 7.1 fusion.20
  380.9 5.9 copy.69
  386.8 4.7 fusion.23
  391.7 92.3 %all-reduce.7.cloned.1.call-done = bf16[5,512,512]{2,1,0:T(8,128)(2,1)} async-done(((bf16[5,512,512]{2,1,0:T(8,128)(2,1)}), bf16[5,512,512]{2,1,0:T(8,128)(2,1)}) %all-reduce.7.cloned.1.call-update) | async-done | bytes 2621456 | tf_op jit(solution)/shard_map/psum | solution.py:15
  489.9 49.6 %all-gather.15.cloned.1.call-done = bf16[16,512,512]{2,1,0:T(8,128)(2,1)} async-done(((bf16[2,512,512]{2,1,0:T(8,128)(2,1)}), bf16[16,512,512]{2,1,0:T(8,128)(2,1)}) %all-gather.15.cloned.1.call-update) | async-done | bytes 8388624 | tf_op jit(solution)/shard_map/all_gather | solution.py:10
  539.5 4.3 bitcast_subtract_fusion
  547.4 49.6 %all-gather.11.cloned.1.call-done = f32[8,512,512]{2,1,0:T(8,128)} async-done(((f32[1,512,512]{2,1,0:T(8,128)}), f32[8,512,512]{2,1,0:T(8,128)}) %all-gather.11.cloned.1.call-update) | async-done | bytes 8388624 | tf_op jit(solution)/shard_map/all_gather | solution.py:10
  599.3 11.7 %cholesky.358 = f32[128,128]{1,0:T(8,128)S(1)} custom-call(f32[128,128]{1,0:T(8,128)S(1)} %cholesky.439), custom_call_target="Cholesky" | custom-call | tf_op jit(solution)/shard_map/jit(cholesky)/cholesky | solution.py:36
  611.2 9.8 %custom-call.35 = f32[1,128,128]{1,2,0:T(8,128)S(1)} custom-call(f32[1,128,128]{2,1,0:T(8,128)S(1)} %get-tuple-element.57), custom_call_target="InvertDiagBlocksLowerTriangular" | custom-call | tf_op jit(solution)/shard_map/jit(cholesky)/cholesky | solution.py:36
  623.5 11.7 %cholesky.377 = f32[128,128]{1,0:T(8,128)S(1)} custom-call(f32[128,128]{1,0:T(8,128)S(1)} %cholesky.443), custom_call_target="Cholesky" | custom-call | tf_op jit(solution)/shard_map/jit(cholesky)/cholesky | solution.py:36
  635.3 10.2 %custom-call.36 = f32[1,128,128]{1,2,0:T(8,128)S(1)} custom-call(f32[1,128,128]{2,1,0:T(8,128)S(1)} %get-tuple-element.54), custom_call_target="InvertDiagBlocksLowerTriangular" | custom-call | tf_op jit(solution)/shard_map/jit(cholesky)/cholesky | solution.py:36
  647.1 11.7 %cholesky.398 = f32[128,128]{1,0:T(8,128)S(1)} custom-call(f32[128,128]{1,0:T(8,128)S(1)} %cholesky.448), custom_call_target="Cholesky" | custom-call | tf_op jit(solution)/shard_map/jit(cholesky)/cholesky | solution.py:36
  658.8 9.8 %custom-call.37 = f32[1,128,128]{1,2,0:T(8,128)S(1)} custom-call(f32[1,128,128]{2,1,0:T(8,128)S(1)} %get-tuple-element.51), custom_call_target="InvertDiagBlocksLowerTriangular" | custom-call | tf_op jit(solution)/shard_map/jit(cholesky)/cholesky | solution.py:36
  670.1 11.8 %cholesky.415 = f32[128,128]{1,0:T(8,128)S(1)} custom-call(f32[128,128]{1,0:T(8,128)S(1)} %convolution_subtract_fusion.8), custom_call_target="Cholesky" | custom-call | tf_op jit(solution)/shard_map/jit(cholesky)/cholesky | solution.py:36
  688.3 8.1 while.5
  696.4 39.3 %custom-call.38 = f32[4,128,128]{1,2,0:T(8,128)S(1)} custom-call(f32[4,128,128]{2,1,0:T(8,128)S(1)} %get-tuple-element.23), custom_call_target="InvertDiagBlocksLowerTriangular" | custom-call | tf_op jit(solution)/shard_map/triangular_solve/custom-call.3 | solution.py:37
  743.4 4.4 convolution_subtract_fusion.2
  749.1 6.9 fusion.17
  759.9 5.9 copy.72
  765.8 4.8 fusion.24
  770.7 92.4 %all-reduce.9.cloned.1.call-done = bf16[5,512,512]{2,1,0:T(8,128)(2,1)} async-done(((bf16[5,512,512]{2,1,0:T(8,128)(2,1)}), bf16[5,512,512]{2,1,0:T(8,128)(2,1)}) %all-reduce.9.cloned.1.call-update) | async-done | bytes 2621456 | tf_op jit(solution)/shard_map/psum | solution.py:15
  870.2 9.0 gather_fusion.1
  881.5 5.0 fusion.48
  886.5 8.5 gather_fusion
  895.2 21.1 %all-gather.17.cloned.1.call-done = bf16[16,512,512]{2,1,0:T(8,128)(2,1)} async-done(((bf16[2,512,512]{2,1,0:T(8,128)(2,1)}), bf16[16,512,512]{2,1,0:T(8,128)(2,1)}) %all-gather.17.cloned.1.call-update) | async-done | bytes 8388624 | tf_op jit(solution)/shard_map/all_gather | solution.py:10
  916.4 9.3 fusion.4
  925.7 7.2 select_bitcast_fusion
  932.9 6.3 maximum_bitcast_fusion
  939.3 20.1 %copy.73 = f32[5,1,512,2,1,512]{5,4,3,2,1,0:T(1,128)} copy(f32[5,1,512,2,1,512]{5,2,0,3,4,1:T(8,128)S(1)} %maximum_bitcast_fusion) | data formatting | bytes 20971520 | tf_op jit(solution)/shard_map/broadcast_in_dim | solution.py:127
  (176 shorter events, 93.5 us)
Async XLA Ops:
  7.4 92.9 %copy-start = (f32[32,512]{1,0:T(8,128)S(1)}, f32[32,512]{1,0:T(8,128)}, u32[]{:S(2)}) copy-start(f32[32,512]{1,0:T(8,128)} %param.12) | copy-start | bytes 196612
  7.4 88.9 %reduce-scatter.2.cloned.1.call-start = ((), (), s32[]{:S(2)}) async-start(), calls=%async_computation.1 | async-start | bytes 5570560 | tf_op jit(solution)/shard_map/reduce_scatter | solution.py:26
  14.8 1.7 copy-start.9
  14.8 94.4 %all-reduce.5.cloned.1.call-start = ((), (), s32[]{:S(2)}) async-start(), calls=%async_computation.3 | async-start | bytes 4194304 | tf_op jit(solution)/shard_map/psum | solution.py:85
  19.4 135.9 %all-gather.9.cloned.1.call-start = ((), (), s32[]{:S(2)}) async-start(), calls=%async_computation.2 | async-start | bytes 5570560 | tf_op jit(solution)/shard_map/all_gather | solution.py:27
  96.3 121.7 %all-gather.13.cloned.1.call-start = ((), (), s32[]{:S(2)}) async-start(), calls=%async_computation.7 | async-start | bytes 9437184 | tf_op jit(solution)/shard_map/all_gather | solution.py:10
  97.4 6.1 copy-start.7
  100.1 3.4 copy-start.10
  163.2 4.1 copy-start.2
  168.3 315.7 %all-reduce.7.cloned.1.call-start = ((), (), s32[]{:S(2)}) async-start(), calls=%async_computation.4 | async-start | bytes 5242880 | tf_op jit(solution)/shard_map/psum | solution.py:15
  218.0 1.2 slice-start.6
  220.2 11.7 %copy-start.11 = (f32[512,512]{1,0:T(8,128)}, f32[512,512]{1,0:T(8,128)S(1)}, u32[]{:S(2)}) copy-start(f32[512,512]{1,0:T(8,128)S(1)} %fusion.43) | copy-start | bytes 3145732
  307.6 56.6 %slice-start.4 = ((s8[5242880]{0:T(1024)(128)(4,1)}), s8[1048576]{0:T(1024)(128)(4,1)S(1)}, s32[]{:S(2)}) async-start(s8[5242880]{0:T(1024)(128)(4,1)} %bitcast.208), calls=%async_computation.14 | async-start | bytes 2097152
  356.6 7.6 slice-start.5
  391.6 147.9 %all-gather.15.cloned.1.call-start = ((), (), s32[]{:S(2)}) async-start(), calls=%async_computation.8 | async-start | bytes 9437184 | tf_op jit(solution)/shard_map/all_gather | solution.py:10
  484.0 55.5 %copy-start.4 = (bf16[5,512,512]{2,1,0:T(8,128)(2,1)S(1)}, bf16[5,512,512]{2,1,0:T(8,128)(2,1)}, u32[]{:S(2)}) copy-start(bf16[5,512,512]{2,1,0:T(8,128)(2,1)} %all-reduce.7.cloned.1.call-done) | copy-start | bytes 7864324
  489.9 107.2 %all-gather.11.cloned.1.call-start = ((), (), s32[]{:S(2)}) async-start(), calls=%async_computation.5 | async-start | bytes 9437184 | tf_op jit(solution)/shard_map/all_gather | solution.py:10
  543.8 2.4 copy-start.3
  547.2 315.9 %all-reduce.9.cloned.1.call-start = ((), (), s32[]{:S(2)}) async-start(), calls=%async_computation.6 | async-start | bytes 5242880 | tf_op jit(solution)/shard_map/psum | solution.py:15
  597.0 1.2 slice-start.7
  599.3 11.7 %copy-start.12 = (f32[512,512]{1,0:T(8,128)}, f32[512,512]{1,0:T(8,128)S(1)}, u32[]{:S(2)}) copy-start(f32[512,512]{1,0:T(8,128)S(1)} %fusion.42) | copy-start | bytes 3145732
  687.0 56.3 %slice-start = ((s8[5242880]{0:T(1024)(128)(4,1)}), s8[1048576]{0:T(1024)(128)(4,1)S(1)}, s32[]{:S(2)}) async-start(s8[5242880]{0:T(1024)(128)(4,1)} %bitcast.197), calls=%async_computation.10 | async-start | bytes 2097152
  735.7 7.6 slice-start.1
  770.7 145.7 %all-gather.17.cloned.1.call-start = ((), (), s32[]{:S(2)}) async-start(), calls=%async_computation.9 | async-start | bytes 9437184 | tf_op jit(solution)/shard_map/all_gather | solution.py:10
  866.7 14.8 %copy-start.5 = (bf16[5,512,512]{2,1,0:T(8,128)(2,1)S(1)}, bf16[5,512,512]{2,1,0:T(8,128)(2,1)}, u32[]{:S(2)}) copy-start(bf16[5,512,512]{2,1,0:T(8,128)(2,1)} %all-reduce.7.cloned.1.call-done) | copy-start | bytes 7864324
  886.5 8.5 copy-start.6
  895.0 30.7 %slice-start.2 = ((s8[5242880]{0:T(1024)(128)(4,1)}), s8[1048576]{0:T(1024)(128)(4,1)S(1)}, s32[]{:S(2)}) async-start(s8[5242880]{0:T(1024)(128)(4,1)} %bitcast.201), calls=%async_computation.12 | async-start | bytes 2097152
  916.3 9.4 slice-start.3
  916.3 9.4 copy-start.8
  916.3 9.4 copy-start.13
  939.3 20.1 %copy-start.1 = (f32[32,512]{1,0:T(8,128)S(1)}, f32[32,512]{1,0:T(8,128)}, u32[]{:S(2)}) copy-start(f32[32,512]{1,0:T(8,128)} %param.12) | copy-start | bytes 196612
Sparse Core Ops, SparseCore 0:
  14.9 81.2 reduce-scatter.1
  98.4 56.8 all-gather.8
  391.7 92.2 all-reduce.6
  770.8 92.2 all-reduce.8
Sparse Core Ops, SparseCore 1:
  19.5 66.9 all-reduce.4
  168.4 49.5 all-gather.12
  489.9 49.5 all-gather.14
  547.3 49.7 all-gather.10
  866.8 49.5 all-gather.16
where the time goes:
time: 973 us; the launch traced here: 967 us
  waiting for transfers between devices  472 us (49%)
  other arithmetic  281 us (29%)
  local copies, waits for them, and re-layouts  95.8 us (10%)
  matrix products  95.2 us (10%)
  between operations  22.5 us (2%)
    psum x2, waiting for transfers between devices, spread(): return lax.psum(jnp.where(mine, value, jnp.zeros_like(value)), axis)  185 us
    all_gather x4, waiting for transfers between devices, from_root(): lax.all_gather(value, axis)  164 us
    another operation x29, other arithmetic, factor_panel(): factor = jnp.linalg.cholesky(pivot_tile)  159 us
    another operation x7, other arithmetic, factor_panel(): lax.linalg.triangular_solve(factor, column.reshape(-1, extent), left_side...  86.3 us
    reduce_scatter x1, waiting for transfers between devices, sum_by_parts(): own = lax.psum_scatter(padded, axis, scatter_dimension=0, tiled=True)  76.8 us
    all_gather x1, waiting for transfers between devices, sum_by_parts(): whole = lax.all_gather(own, axis, axis=0, tiled=True)  46.1 us
    another operation x14, matrix products, factor_panel(): lax.linalg.triangular_solve(factor, column.reshape(-1, extent), left_side...  43.2 us
    another operation x29, local copies, waits for them, and re-layouts, factor_panel(): lax.linalg.triangular_solve(factor, column.reshape(-1, extent), left_side...  28.1 us
  transfers between devices with their start and end apart: 9, of which 8 were waited for; matrix products, arithmetic and copies ran while one was open for 5% of the time, Pallas kernels for 0%

commit v1 on v0

--- a/solution.py
+++ b/solution.py
@@ -2,6 +2,7 @@
 import jax.numpy as jnp
 from jax import lax
 from jax.sharding import PartitionSpec as P
+from jax.lax import all_gather
 
 PANELS = 2
 
@@ -12,7 +13,7 @@
 
 def spread(value, axis, root):
     mine = lax.axis_index(axis) == root
-    return lax.psum(jnp.where(mine, value, jnp.zeros_like(value)), axis)
+    return jnp.sum(all_gather(jnp.where(mine, value, jnp.zeros_like(value)), axis), 0)
 
 
 def rows_for(lines, size):

time: 973 us -> 1320 us (1.36)
  waiting for transfers between devices: 472 us -> 767 us
  other arithmetic: 281 us -> 319 us
    all_gather x0 -> x2, waiting for transfers between devices: none -> 480 us  [spread(): all_gather(jnp.where(mine, value, jnp.zeros_like(value)), axis)]
    psum x2 -> x0, waiting for transfers between devices: 185 us -> none  [spread(): return lax.psum(jnp.where(mine, value, jnp.zeros_like(value)), axis)]
    reduce_sum x0 -> x2, other arithmetic: none -> 30.1 us  [spread(): jnp.sum(all_gather(jnp.where(mine, value, jnp.zeros_like(value)), axis), 0)]
  transfers between devices with their start and end apart: 9 -> 9, of which waited for: 8 -> 8; matrix products, arithmetic and copies ran while one was open for 5% -> 4% of each run, Pallas kernels for 0% -> 0%
where the time goes in v1:
time: 1320 us
  waiting for transfers between devices  767 us (58%)
  other arithmetic  319 us (24%)
  local copies, waits for them, and re-layouts  106 us (8%)
  matrix products  100 us (8%)
  between operations  22.2 us (2%)
    all_gather x2, waiting for transfers between devices, spread(): all_gather(jnp.where(mine, value, jnp.zeros_like(value)), axis)  480 us
    all_gather x4, waiting for transfers between devices, from_root(): lax.all_gather(value, axis)  164 us
    another operation x29, other arithmetic, factor_panel(): factor = jnp.linalg.cholesky(pivot_tile)  160 us
    another operation x7, other arithmetic, factor_panel(): lax.linalg.triangular_solve(factor, column.reshape(-1, extent), left_side...  87.7 us
    reduce_scatter x1, waiting for transfers between devices, sum_by_parts(): own = lax.psum_scatter(padded, axis, scatter_dimension=0, tiled=True)  76.7 us
    all_gather x1, waiting for transfers between devices, sum_by_parts(): whole = lax.all_gather(own, axis, axis=0, tiled=True)  46 us
    another operation x14, matrix products, factor_panel(): lax.linalg.triangular_solve(factor, column.reshape(-1, extent), left_side...  45.9 us
    another operation x29, local copies, waits for them, and re-layouts, factor_panel(): lax.linalg.triangular_solve(factor, column.reshape(-1, extent), left_side...  31.6 us
  transfers between devices with their start and end apart: 9, of which 8 were waited for; matrix products, arithmetic and copies ran while one was open for 4% of the time, Pallas kernels for 0%

profile of v1, /device:TPU:1, one launch (start us, length us, event | category | flops | bytes accessed | tf_op | source)
XLA Modules:
  0.0 1315.2 jit_solution(11130379635255964868)
XLA Ops:
  8.3 6.5 fusion.31
  19.4 76.7 %reduce-scatter.2.cloned.1.call-done = f32[160,512]{1,0:T(8,128)} async-done(((f32[2560,512]{1,0:T(8,128)}), f32[160,512]{1,0:T(8,128)}) %reduce-scatter.2.cloned.1.call-update) | async-done | bytes 327696 | tf_op jit(solution)/shard_map/reduce_scatter | solution.py:27
  103.4 5.7 fusion.32
  109.1 46.0 %all-gather.11.cloned.1.call-done = f32[2560,512]{1,0:T(8,128)} async-done(((f32[160,512]{1,0:T(8,128)}), f32[2560,512]{1,0:T(8,128)}) %all-gather.11.cloned.1.call-update) | async-done | bytes 5242896 | tf_op jit(solution)/shard_map/all_gather | solution.py:28
  155.1 7.9 bitcast_add_fusion
  168.4 5.8 slice.199
  174.3 43.5 %all-gather.19.cloned.1.call-done = f32[8,1,512,512]{3,2,1,0:T(8,128)} async-done(((f32[1,1,512,512]{3,2,1,0:T(8,128)}), f32[8,1,512,512]{3,2,1,0:T(8,128)}) %all-gather.19.cloned.1.call-update) | async-done | bytes 8388624 | tf_op jit(solution)/shard_map/all_gather | solution.py:11
  220.1 11.7 cholesky.286
  231.9 9.8 custom-call.31
  244.3 11.7 cholesky.305
  256.0 10.3 custom-call.32
  267.9 11.7 cholesky.326
  279.6 9.8 custom-call.33
  290.9 11.9 cholesky.343
  308.7 8.3 while.4
  317.1 39.3 %custom-call.34 = f32[4,128,128]{1,2,0:T(8,128)S(1)} custom-call(f32[4,128,128]{2,1,0:T(8,128)S(1)} %get-tuple-element.22), custom_call_target="InvertDiagBlocksLowerTriangular" | custom-call | tf_op jit(solution)/shard_map/triangular_solve/custom-call.3 | solution.py:38
  364.1 4.4 convolution_subtract_fusion.3
  369.8 7.1 fusion.20
  380.7 5.9 copy.59
  386.6 4.8 fusion.23
  391.5 239.9 %all-gather.13.cloned.1.call-done = bf16[16,5,512,512]{3,2,1,0:T(8,128)(2,1)} async-done(((bf16[1,5,512,512]{3,2,1,0:T(8,128)(2,1)}), bf16[16,5,512,512]{3,2,1,0:T(8,128)(2,1)}) %all-gather.13.cloned.1.call-update) | async-done | bytes 41943056 | tf_op jit(solution)/shard_map/all_gather | solution.py:16
  631.5 14.2 %reduce_sum.24 = bf16[5,512,512]{2,1,0:T(8,128)(2,1)S(1)} reduce(bf16[16,5,512,512]{3,2,1,0:T(8,128)(2,1)} %all-gather.13.cloned.1.call-done, bf16[]{:T(256)} %constant.183.clone.1), dimensions={0}, to_apply=%region_10.13 | reduce | flops 19660800 | bytes 44564480 | tf_op jit(solution)/shard_map/reduce_sum | solution.py:16
  649.6 49.6 %all-gather.21.cloned.1.call-done = bf16[16,512,512]{2,1,0:T(8,128)(2,1)} async-done(((bf16[2,512,512]{2,1,0:T(8,128)(2,1)}), bf16[16,512,512]{2,1,0:T(8,128)(2,1)}) %all-gather.21.cloned.1.call-update) | async-done | bytes 8388624 | tf_op jit(solution)/shard_map/all_gather | solution.py:11
  699.2 4.3 bitcast_subtract_fusion
  707.1 49.6 %all-gather.15.cloned.1.call-done = f32[8,512,512]{2,1,0:T(8,128)} async-done(((f32[1,512,512]{2,1,0:T(8,128)}), f32[8,512,512]{2,1,0:T(8,128)}) %all-gather.15.cloned.1.call-update) | async-done | bytes 8388624 | tf_op jit(solution)/shard_map/all_gather | solution.py:11
  769.1 11.7 cholesky.358
  782.0 9.8 custom-call.35
  795.0 11.7 cholesky.377
  807.3 10.2 custom-call.36
  819.9 11.7 cholesky.398
  832.3 9.8 custom-call.37
  844.3 11.8 cholesky.415
  864.7 11.6 while.5
  876.2 39.3 %custom-call.38 = f32[4,128,128]{1,2,0:T(8,128)S(1)} custom-call(f32[4,128,128]{2,1,0:T(8,128)S(1)} %get-tuple-element.23), custom_call_target="InvertDiagBlocksLowerTriangular" | custom-call | tf_op jit(solution)/shard_map/triangular_solve/custom-call.3 | solution.py:38
  923.1 5.8 convolution_subtract_fusion.2
  930.2 8.3 fusion.17
  942.3 5.9 copy.62
  948.2 4.8 fusion.24
  953.1 240.0 %all-gather.17.cloned.1.call-done = bf16[16,5,512,512]{3,2,1,0:T(8,128)(2,1)} async-done(((bf16[1,5,512,512]{3,2,1,0:T(8,128)(2,1)}), bf16[16,5,512,512]{3,2,1,0:T(8,128)(2,1)}) %all-gather.17.cloned.1.call-update) | async-done | bytes 41943056 | tf_op jit(solution)/shard_map/all_gather | solution.py:16
  1193.1 15.9 %reduce_sum.25 = bf16[5,512,512]{2,1,0:T(8,128)(2,1)} reduce(bf16[16,5,512,512]{3,2,1,0:T(8,128)(2,1)} %all-gather.17.cloned.1.call-done, bf16[]{:T(256)} %constant.183.clone.1), dimensions={0}, to_apply=%region_11.15 | reduce | flops 19660800 | bytes 44564480 | tf_op jit(solution)/shard_map/reduce_sum | solution.py:16
  1218.0 8.7 gather_fusion.1
  1229.1 5.0 fusion.48
  1234.1 8.7 gather_fusion
  1243.0 21.4 %all-gather.23.cloned.1.call-done = bf16[16,512,512]{2,1,0:T(8,128)(2,1)} async-done(((bf16[2,512,512]{2,1,0:T(8,128)(2,1)}), bf16[16,512,512]{2,1,0:T(8,128)(2,1)}) %all-gather.23.cloned.1.call-update) | async-done | bytes 8388624 | tf_op jit(solution)/shard_map/all_gather | solution.py:11
  1264.4 9.3 fusion.4
  1273.8 7.2 select_bitcast_fusion
  1281.0 6.3 maximum_bitcast_fusion
  1287.3 20.1 %copy.65 = f32[5,1,512,2,1,512]{5,4,3,2,1,0:T(1,128)} copy(f32[5,1,512,2,1,512]{5,2,0,3,4,1:T(8,128)S(1)} %maximum_bitcast_fusion) | data formatting | bytes 20971520 | tf_op jit(solution)/shard_map/broadcast_in_dim | solution.py:128
  (168 shorter events, 121.4 us)
Async XLA Ops:
  7.4 92.7 %copy-start = (f32[32,512]{1,0:T(8,128)S(1)}, f32[32,512]{1,0:T(8,128)}, u32[]{:S(2)}) copy-start(f32[32,512]{1,0:T(8,128)} %param.12) | copy-start | bytes 196612
  7.4 88.7 %reduce-scatter.2.cloned.1.call-start = ((), (), s32[]{:S(2)}) async-start(), calls=%async_computation.1 | async-start | bytes 5570560 | tf_op jit(solution)/shard_map/reduce_scatter | solution.py:27
  14.7 1.7 copy-start.7
  14.7 94.3 %all-reduce.3.cloned.1.call-start = ((), (), s32[]{:S(2)}) async-start(), calls=%async_computation.3 | async-start | bytes 4194304 | tf_op jit(solution)/shard_map/psum | solution.py:86
  19.4 135.7 %all-gather.11.cloned.1.call-start = ((), (), s32[]{:S(2)}) async-start(), calls=%async_computation.2 | async-start | bytes 5570560 | tf_op jit(solution)/shard_map/all_gather | solution.py:28
  96.1 121.6 %all-gather.19.cloned.1.call-start = ((), (), s32[]{:S(2)}) async-start(), calls=%async_computation.7 | async-start | bytes 9437184 | tf_op jit(solution)/shard_map/all_gather | solution.py:11
  97.3 6.1 copy-start.6
  100.0 3.4 copy-start.8
  163.0 4.1 copy-start.2
  168.1 463.3 %all-gather.13.cloned.1.call-start = ((), (), s32[]{:S(2)}) async-start(), calls=%async_computation.4 | async-start | bytes 44564480 | tf_op jit(solution)/shard_map/all_gather | solution.py:16
  217.8 1.2 slice-start.4
  220.0 11.7 copy-start.9
  307.4 56.6 %slice-start.2 = ((s8[5242880]{0:T(1024)(128)(4,1)}), s8[1048576]{0:T(1024)(128)(4,1)S(1)}, s32[]{:S(2)}) async-start(s8[5242880]{0:T(1024)(128)(4,1)} %bitcast.208), calls=%async_computation.12 | async-start | bytes 2097152
  356.4 7.6 slice-start.3
  391.4 307.8 %all-gather.21.cloned.1.call-start = ((), (), s32[]{:S(2)}) async-start(), calls=%async_computation.8 | async-start | bytes 9437184 | tf_op jit(solution)/shard_map/all_gather | solution.py:11
  649.6 107.1 %all-gather.15.cloned.1.call-start = ((), (), s32[]{:S(2)}) async-start(), calls=%async_computation.5 | async-start | bytes 9437184 | tf_op jit(solution)/shard_map/all_gather | solution.py:11
  703.5 2.3 copy-start.3
  706.9 486.2 %all-gather.17.cloned.1.call-start = ((), (), s32[]{:S(2)}) async-start(), calls=%async_computation.6 | async-start | bytes 44564480 | tf_op jit(solution)/shard_map/all_gather | solution.py:16
  768.1 1.0 copy-start.10
  953.0 311.4 %all-gather.23.cloned.1.call-start = ((), (), s32[]{:S(2)}) async-start(), calls=%async_computation.9 | async-start | bytes 9437184 | tf_op jit(solution)/shard_map/all_gather | solution.py:11
  1234.1 8.7 copy-start.4
  1242.8 30.9 %slice-start = ((s8[5242880]{0:T(1024)(128)(4,1)}), s8[1048576]{0:T(1024)(128)(4,1)S(1)}, s32[]{:S(2)}) async-start(s8[5242880]{0:T(1024)(128)(4,1)} %bitcast.201), calls=%async_computation.10 | async-start | bytes 2097152
  1264.4 9.4 slice-start.1
  1264.4 9.4 copy-start.5
  1264.4 9.4 copy-start.11
  1287.3 20.1 %copy-start.1 = (f32[32,512]{1,0:T(8,128)S(1)}, f32[32,512]{1,0:T(8,128)}, u32[]{:S(2)}) copy-start(f32[32,512]{1,0:T(8,128)} %param.12) | copy-start | bytes 196612
Sparse Core Ops, SparseCore 0:
  14.9 81.1 reduce-scatter.1
  98.2 56.8 all-gather.10
  391.5 239.8 all-gather.12
  953.2 239.8 all-gather.16
Sparse Core Ops, SparseCore 1:
  19.4 66.9 all-reduce.2
  168.2 49.5 all-gather.18
  649.6 49.5 all-gather.20
  707.0 49.7 all-gather.14
  1214.8 49.5 all-gather.22
